TPU v7x, 32 devices: a whole 2x2x4 slice. The times are simulated.
32 devices in a mesh: grp: 2 (over x), dev: 16 (over z, y, core).
Axes of the slice: x: 2, y: 2, z: 4, core: 2. Of those that a mesh axis runs over, the one named last changes fastest.
Arguments:
- query: bfloat16 [64, 64, 128], P(('grp', 'dev')), may hold values from -6 to 6
- key_cache: bfloat16 [64, 512, 8, 128], P(('grp', 'dev')), may hold values from -6 to 6
- value_cache: bfloat16 [64, 512, 8, 128], P(('grp', 'dev')), may hold values from -6 to 6
- lengths: int32 [64], P(('grp', 'dev')), may hold values from 1 to 512, 16384 in all
- out_weight: bfloat16 [8192, 8192], P('dev', 'grp'), may hold values from -0.0625 to 0.0625
- resid: bfloat16 [64, 8192], P('dev', 'grp'), may hold values from -6 to 6
- norm_gain: bfloat16 [8192], P('grp'), may hold values from 0.5 to 1.5
- gate_weight: bfloat16 [8192, 28672], P('grp', 'dev'), may hold values from -0.0625 to 0.0625
- up_weight: bfloat16 [8192, 28672], P('grp', 'dev'), may hold values from -0.0625 to 0.0625
- down_weight: bfloat16 [28672, 8192], P('dev', 'grp'), may hold values from -0.03125 to 0.03125
Outputs:
- layer_out: bfloat16 [64, 8192], P('dev', 'grp')
Inputs may be any that keep to these rules, and one draw needn't show every extreme that they name: `lengths`: some request has exactly 512 live slots.
All inputs are finite; a program needn't handle non-finite values. No bound on the sum of `lengths` on one device may be relied on, other than what follows from the above.
Results may differ from a plain program's by a relative error of at most 0.015.
Values may be sent and summed in bfloat16 or wider, within the bound.
A program may use at most 128 MiB of HBM per device.

v0:
```python
import jax
import jax.numpy as jnp
from jax import lax
from jax.sharding import PartitionSpec as P


def attend(query, key_cache, value_cache, lengths):
    rows, heads, width = query.shape
    kv_heads = key_cache.shape[2]
    group = heads // kv_heads
    grouped = query.reshape(rows, kv_heads, group, width)
    scores = jnp.einsum(
        "rhgd,rlhd->rhgl", grouped, key_cache, preferred_element_type=jnp.float32
    ) * width ** (-0.5)
    places = jnp.arange(key_cache.shape[1], dtype=jnp.int32)
    valid = places[None, :] < lengths[:, None]
    scores = jnp.where(valid[:, None, None, :], scores, -1e30)
    top = jnp.max(scores, axis=-1, keepdims=True)
    weights = jnp.exp(scores - top)
    probs = (weights / jnp.sum(weights, axis=-1, keepdims=True)).astype(jnp.bfloat16)
    mixed = jnp.einsum("rhgl,rlhd->rhgd", probs, value_cache, preferred_element_type=jnp.float32)
    return mixed.reshape(rows, heads * width).astype(jnp.bfloat16)


def per_device(
    query,
    key_cache,
    value_cache,
    lengths,
    out_weight,
    resid,
    norm_gain,
    gate_weight,
    up_weight,
    down_weight,
):
    attn = attend(query, key_cache, value_cache, lengths)
    block_cols = out_weight.shape[0]
    first_col = lax.axis_index("dev") * block_cols
    cols = lax.dynamic_slice_in_dim(
        lax.all_gather(attn, ("grp", "dev"), axis=0, tiled=True), first_col, block_cols, 1
    )
    proj_terms = jnp.dot(cols, out_weight, preferred_element_type=jnp.float32)
    x = resid.astype(jnp.float32) + lax.psum_scatter(
        proj_terms, "dev", scatter_dimension=0, tiled=True
    )
    width_all = x.shape[1] * lax.axis_size("grp")
    sumsq = lax.psum(jnp.sum(x * x, axis=1), "grp")
    normed = (
        x * lax.rsqrt(sumsq / width_all + 1e-05)[:, None] * norm_gain.astype(jnp.float32)
    ).astype(jnp.bfloat16)
    piece = lax.all_gather(normed, "dev", axis=0, tiled=True)
    half_terms = jnp.concatenate(
        [
            jnp.dot(piece, gate_weight, preferred_element_type=jnp.float32),
            jnp.dot(piece, up_weight, preferred_element_type=jnp.float32),
        ],
        axis=1,
    )
    both = lax.psum(half_terms.astype(jnp.bfloat16), "grp").astype(jnp.float32)
    hidden_cols = gate_weight.shape[1]
    gate = both[:, :hidden_cols]
    up = both[:, hidden_cols:]
    hidden = (jax.nn.silu(gate) * up).astype(jnp.bfloat16)
    ffn_rows = lax.psum_scatter(
        jnp.dot(hidden, down_weight, preferred_element_type=jnp.float32),
        "dev",
        scatter_dimension=0,
        tiled=True,
    )
    return (x + ffn_rows).astype(jnp.bfloat16)


def solution(mesh):
    placed = (
        P(("grp", "dev"), None, None),
        P(("grp", "dev"), None, None, None),
        P(("grp", "dev"), None, None, None),
        P(("grp", "dev")),
        P("dev", "grp"),
        P("dev", "grp"),
        P("grp"),
        P("grp", "dev"),
        P("grp", "dev"),
        P("dev", "grp"),
    )
    return jax.shard_map(
        per_device, mesh=mesh, in_specs=placed, out_specs=P("dev", "grp"), check_vma=False
    )
```

profile of v0, /device:TPU:0, one launch (start us, length us, event | category | flops | bytes accessed | tf_op | source)
XLA Modules:
  0.0 347.9 jit_solution(15746743131024164946)
XLA Ops:
  6.5 0.9 iota_compare_fusion
  7.4 0.7 copy-done
  8.1 1.4 fusion.10
  9.6 0.2 fusion.28
  9.8 2.1 fusion.13
  11.9 0.6 reshape.27
  12.5 0.0 all-gather.4.cloned.1.call-update
  12.6 0.0 all-reduce.8.cloned.1.call-start
  12.6 0.0 copy-start.3
  12.7 56.5 %all-gather.4.cloned.1.call-done = bf16[32,2,8192]{2,1,0:T(2,128)(2,1)} async-done(((bf16[1,2,8192]{2,1,0:T(2,128)(2,1)}), bf16[32,2,8192]{2,1,0:T(2,128)(2,1)}) %all-gather.4.cloned.1.call-update) | async-done | bytes 1048592 | tf_op jit(solution)/shard_map/all_gather | solution.py:41
  69.1 1.5 reshape.28
  70.6 4.1 %fusion.22 = f32[64,4096]{1,0:T(8,128)} fusion(bf16[512,4096]{1,0:T(8,128)(2,1)} %param.14, bf16[64,8192]{1,0:T(8,128)(2,1)S(1)} %reshape.28, s32[]{:T(128)S(6)} %select_n.8), kind=kOutput, calls=%fused_computation.24 | convolution fusion | flops 268435456 | bytes 5308420 | tf_op jit(solution)/shard_map/dot_general | solution.py:43
  74.7 0.0 all-reduce.8.cloned.1.call-update
  74.7 0.0 all-reduce.6.cloned.1.call-start
  74.8 0.6 dynamic-slice
  76.0 91.0 %all-reduce.8.cloned.1.call-done = f32[64,4096]{1,0:T(8,128)} async-done(((f32[64,4096]{1,0:T(8,128)}), f32[64,4096]{1,0:T(8,128)}) %all-reduce.8.cloned.1.call-update) | async-done | bytes 1048592
  167.0 1.1 multiply_reduce_fusion
  168.1 4.9 %psum.14 = f32[4]{0:T(128)S(1)} all-reduce(f32[4]{0:T(128)S(1)} %multiply_reduce_fusion), channel_id=1, replica_groups=mesh['grp'=2,'dev'=16] {'grp'}, use_global_device_ids=true, to_apply=%region_4.5 | all-reduce | flops 4 | bytes 32 | tf_op jit(solution)/shard_map/psum | solution.py:48
  173.0 1.0 fusion.24
  174.0 21.1 %all-gather.1 = bf16[16,4,4096]{2,1,0:T(4,128)(2,1)S(1)} all-gather(bf16[1,4,4096]{2,1,0:T(4,128)(2,1)S(1)} %fusion.24), channel_id=1, replica_groups=mesh['grp'=2,'dev'=16] {'dev'}, dimensions={0}, use_global_device_ids=true | all-gather | bytes 557056 | tf_op jit(solution)/shard_map/all_gather | solution.py:52
  195.1 0.1 reshape.30
  195.2 7.8 %convolution_convert_fusion = bf16[64,1792]{1,0:T(8,128)(2,1)S(1)} fusion(bf16[64,4096]{1,0:T(8,128)(2,1)S(1)} %reshape.30, bf16[4096,1792]{1,0:T(8,128)(2,1)} %param.18), kind=kOutput, calls=%fused_computation.1 | convolution fusion | flops 939638784 | bytes 15433728 | tf_op jit(solution)/shard_map/dot_general | solution.py:56
  203.0 7.8 %convolution_convert_fusion.1 = bf16[64,1792]{1,0:T(8,128)(2,1)S(1)} fusion(bf16[64,4096]{1,0:T(8,128)(2,1)S(1)} %reshape.30, bf16[4096,1792]{1,0:T(8,128)(2,1)} %param.17), kind=kOutput, calls=%fused_computation.2 | convolution fusion | flops 939638784 | bytes 15433728 | tf_op jit(solution)/shard_map/dot_general | solution.py:55
  210.8 0.8 pad_maximum_fusion
  211.6 0.0 all-reduce.6.cloned.1.call-update
  211.7 0.0 all-reduce.10.cloned.1.call-start
  211.7 24.5 %all-reduce.6.cloned.1.call-done = bf16[64,3584]{1,0:T(8,128)(2,1)} async-done(((bf16[64,3584]{1,0:T(8,128)(2,1)}), bf16[64,3584]{1,0:T(8,128)(2,1)}) %all-reduce.6.cloned.1.call-update) | async-done | bytes 458768 | tf_op jit(solution)/shard_map/psum | solution.py:60
  236.3 1.1 convert_element_type.34
  237.3 8.8 %fusion.17 = f32[64,4096]{1,0:T(8,128)} fusion(bf16[1792,4096]{1,0:T(8,128)(2,1)} %param.19, f32[64,3584]{1,0:T(8,128)S(1)} %convert_element_type.34), kind=kOutput, calls=%fused_computation.16 | convolution fusion | flops 940212224 | bytes 16646144 | tf_op jit(solution)/shard_map/dot_general | solution.py:66
  246.2 0.0 all-reduce.10.cloned.1.call-update
  246.2 93.5 %all-reduce.10.cloned.1.call-done = f32[64,4096]{1,0:T(8,128)} async-done(((f32[64,4096]{1,0:T(8,128)}), f32[64,4096]{1,0:T(8,128)}) %all-reduce.10.cloned.1.call-update) | async-done | bytes 1048592
  339.7 1.6 fusion.21
  (9 shorter events, 0.0 us)
Async XLA Ops:
  6.5 1.6 copy-start
  6.5 62.6 %all-gather.4.cloned.1.call-start = ((), (), s32[]{:S(2)}) async-start(), calls=%async_computation.1 | async-start | bytes 1081344 | tf_op jit(solution)/shard_map/all_gather | solution.py:41
  12.6 154.4 %all-reduce.8.cloned.1.call-start = ((), (), s32[]{:S(2)}) async-start(), calls=%async_computation.2 | async-start | bytes 2097152
  12.6 62.1 %copy-start.3 = (u32[32]{0:T(128)S(1)}, u32[32]{0:T(128)}, u32[]{:S(2)}) copy-start(u32[32]{0:T(128)} %constant.33) | copy-start | bytes 388
  12.6 154.4 %copy-start.1 = (bf16[4,4096]{1,0:T(4,128)(2,1)S(1)}, bf16[4,4096]{1,0:T(4,128)(2,1)}, u32[]{:S(2)}) copy-start(bf16[4,4096]{1,0:T(4,128)(2,1)} %param.15) | copy-start | bytes 98308
  12.6 155.4 %copy-start.2 = (bf16[4096]{0:T(1024)(128)(2,1)S(1)}, bf16[4096]{0:T(1024)(128)(2,1)}, u32[]{:S(2)}) copy-start(bf16[4096]{0:T(1024)(128)(2,1)} %param.16) | copy-start | bytes 24580
  74.7 161.6 %all-reduce.6.cloned.1.call-start = ((), (), s32[]{:S(2)}) async-start(), calls=%async_computation | async-start | bytes 917504 | tf_op jit(solution)/shard_map/psum | solution.py:60
  211.7 128.1 %all-reduce.10.cloned.1.call-start = ((), (), s32[]{:S(2)}) async-start(), calls=%async_computation.3 | async-start | bytes 2097152
Sparse Core Ops, SparseCore 0:
  12.7 56.4 all-gather.3
  74.8 92.1 all-reduce.7
  211.8 24.4 all-reduce.5
  246.3 93.3 all-reduce.9
where the time goes:
time: 348 us
  waiting for transfers between devices  266 us (76%)
  matrix products  32.1 us (9%)
  blocking collectives  26 us (7%)
  between operations  13.9 us (4%)
  other arithmetic  6.65 us (2%)
  local copies, waits for them, and re-layouts  3.56 us (1%)
    unnamed x6, waiting for transfers between devices  185 us
    all_gather x1, waiting for transfers between devices, per_device(): lax.all_gather(attn, ('grp', 'dev'), axis=0, tiled=True)  56.5 us
    psum x1, waiting for transfers between devices, per_device(): both = lax.psum(half_terms.astype(jnp.bfloat16), 'grp').astype(jnp.float32)  24.5 us
    all_gather x1, blocking collectives, per_device(): piece = lax.all_gather(normed, 'dev', axis=0, tiled=True)  21.1 us
    dot_general x1, matrix products, per_device(): jnp.dot(hidden, down_weight, preferred_element_type=jnp.float32)  8.84 us
    dot_general x1, matrix products, per_device(): jnp.dot(piece, up_weight, preferred_element_type=jnp.float32)  7.81 us
    dot_general x1, matrix products, per_device(): jnp.dot(piece, gate_weight, preferred_element_type=jnp.float32)  7.81 us
  transfers between devices with their start and end apart: 4, of which 4 were waited for; matrix products, arithmetic and copies ran while one was open for 0% of the time, Pallas kernels for 0%

commit v1 on v0

--- a/solution.py
+++ b/solution.py
@@ -1,7 +1,15 @@
+import functools
+
 import jax
 import jax.numpy as jnp
 from jax import lax
+from jax.experimental import pallas as pl
+from jax.experimental.pallas import tpu as pltpu
 from jax.sharding import PartitionSpec as P
+
+MESH = pl.DeviceIdType.MESH
+F32 = jnp.float32
+BF16 = jnp.bfloat16
 
 
 def attend(query, key_cache, value_cache, lengths):
@@ -71,6 +79,388 @@
     return (x + ffn_rows).astype(jnp.bfloat16)
 
 
+def remote(src, dst, send, recv, **where):
+    return pltpu.make_async_remote_copy(
+        src_ref=src, dst_ref=dst, send_sem=send, recv_sem=recv,
+        device_id=where, device_id_type=MESH,
+    )
+
+
+def loop(n, f):
+    def step(i, carry):
+        f(i)
+        return carry
+
+    lax.fori_loop(0, n, step, 0)
+
+
+def layer_kernel(
+    nd,
+    len_ref, q_ref, k_hbm, v_hbm, wo_hbm, resid_ref, gain_ref, wg_hbm, wu_hbm, wd_hbm,
+    out_ref,
+    kb, vb, wo, wg, wu, wd,
+    sc, ast, abuf, arecv, af, lhs, rbuf,
+    psend, prec, pown, csend, crecv, xf, xall, xg, ssq,
+    gsend, grecv, hid, hcat,
+    psend2, prec2, csend2, crecv2, fin,
+    kvsem, wsem, xs, rs, as_, ar, p1s, p1r, c1s, c1r, ags, agr, fws, fwr,
+    gs, gr, hs, hr, p2s, p2r, c2s, c2r, fs,
+):
+    nc = nd // 2
+    g = lax.axis_index("grp")
+    d = lax.axis_index("dev")
+    c = d // 2
+    k = lax.rem(d, 2)
+    og = 1 - g
+    ok = 1 - k
+    pair = c * 2 + ok
+    rows = nd * 4
+    half = wo.shape[1] // 2
+    nn = half // 512
+    units = wg.shape[1] // 2
+    nu = units // 128
+    heads = q_ref.shape[1]
+    slots = k_hbm.shape[1]
+    width_all = wo.shape[1] * 2
+
+    barrier = pltpu.get_barrier_semaphore()
+    pl.semaphore_signal(barrier, inc=1, device_id={"grp": og}, device_id_type=MESH)
+
+    def greet(i):
+        pl.semaphore_signal(
+            barrier, inc=1, device_id={"dev": lax.rem(d + i + 1, nd)}, device_id_type=MESH
+        )
+
+    loop(nd - 1, greet)
+
+    kv = []
+    for r in range(2):
+        kv.append((
+            pltpu.make_async_copy(k_hbm.at[r], kb.at[r], kvsem.at[2 * r]),
+            pltpu.make_async_copy(v_hbm.at[r], vb.at[r], kvsem.at[2 * r + 1]),
+        ))
+    for a, b in kv:
+        a.start()
+        b.start()
+    wo_copy = pltpu.make_async_copy(wo_hbm, wo, wsem.at[0])
+    wo_copy.start()
+    ucols = [pl.ds(pl.multiple_of(og * units, 128), units), pl.ds(pl.multiple_of(g * units, 128), units)]
+    gu_copies = []
+    for i in range(2):
+        gu_copies.append((
+            pltpu.make_async_copy(wg_hbm.at[:, ucols[i]], wg.at[:, ucols[i]], wsem.at[1 + 2 * i]),
+            pltpu.make_async_copy(wu_hbm.at[:, ucols[i]], wu.at[:, ucols[i]], wsem.at[2 + 2 * i]),
+        ))
+    wd_copy = pltpu.make_async_copy(wd_hbm, wd, wsem.at[5])
+
+    piece = 1024
+    np_ = slots // piece
+    for r in range(2):
+        kv[r][0].wait()
+        q = q_ref[r]
+        length = len_ref[r]
+        row_head = lax.broadcasted_iota(jnp.int32, (heads, piece), 0) // 8
+        col = lax.broadcasted_iota(jnp.int32, (heads, piece), 1)
+        own = lax.rem(col, 8) == row_head
+        place = col // 8
+        top = jnp.full((heads, 1), -1e30, F32)
+        for n in range(np_):
+            s = lax.dot_general(
+                q, kb[r, n * piece:(n + 1) * piece, :], (((1,), (1,)), ((), ())),
+                preferred_element_type=F32,
+            ) * (128 ** -0.5)
+            live = own & (place + n * (piece // 8) < length)
+            s = jnp.where(live, s, -1e30)
+            sc[:, n * piece:(n + 1) * piece] = s
+            top = jnp.maximum(top, jnp.max(s, axis=1, keepdims=True))
+        kv[r][1].wait()
+        if r == 1:
+            for a, b in gu_copies:
+                a.start()
+                b.start()
+            wd_copy.start()
+        total = jnp.zeros((heads, 1), F32)
+        o = jnp.zeros((heads, 128), F32)
+        for n in range(np_):
+            w = jnp.exp(sc[:, n * piece:(n + 1) * piece] - top)
+            total = total + jnp.sum(w, axis=1, keepdims=True)
+            o = o + jnp.dot(w.astype(BF16), vb[r, n * piece:(n + 1) * piece, :], preferred_element_type=F32)
+        o = o / total
+        for t in range(nd):
+            ast[t, 4 * r:4 * r + 4, :] = o[4 * t:4 * t + 4, :]
+    abuf[g] = ast[...].astype(BF16)
+
+    pl.semaphore_wait(barrier, nd)
+    xcopy = remote(abuf.at[g], abuf.at[g], xs.at[0], xs.at[1], grp=og)
+    xcopy.start()
+    rcopy = remote(resid_ref, rbuf.at[k], rs.at[0], rs.at[1], dev=pair)
+    rcopy.start()
+    rbuf[k] = resid_ref[...]
+    xcopy.wait()
+
+    def send_attn(i):
+        to = lax.rem(d + i + 1, nd)
+        remote(abuf.at[:, to], arecv.at[d], as_.at[to], ar.at[d], dev=to).start()
+
+    loop(nd - 1, send_attn)
+    arecv[d] = abuf[:, d]
+
+    def take_attn(i):
+        frm = lax.rem(d + i + 1, nd)
+        remote(abuf.at[:, frm], arecv.at[frm], as_.at[frm], ar.at[frm], dev=frm).wait_recv()
+
+    loop(nd - 1, take_attn)
+    wo_copy.wait()
+    for h in range(2):
+        af[h * nd * 8:(h + 1) * nd * 8, :] = arecv[:, h].astype(F32).reshape(nd * 8, 128)
+    for j in range(4):
+        lhs[:, j * 128:(j + 1) * 128] = af[pl.ds(j, rows, stride=4), :].astype(BF16)
+
+    def reduce_rows(left, w, ps, pr, cs, cr, pss, prs, css, crs, finish):
+        def other(n):
+            cols = pl.ds(pl.multiple_of(ok * half + n * 512, 512), 512)
+            v = jnp.dot(left[...], w[:, cols], preferred_element_type=F32)
+            ps[n] = v.reshape(nc, 8, 512).astype(BF16)
+            remote(ps.at[n], pr.at[n], pss.at[n], prs.at[n], dev=pair).start()
+
+        loop(nn, other)
+
+        def mine(n):
+            cols = pl.ds(pl.multiple_of(k * half + n * 512, 512), 512)
+            v = jnp.dot(left[...], w[:, cols], preferred_element_type=F32)
+            remote(ps.at[n], pr.at[n], pss.at[n], prs.at[n], dev=pair).wait_recv()
+            v = v.reshape(nc, 8, 512) + pr[n].astype(F32)
+            pown[n] = v
+            cs[:, n] = v.astype(BF16)
+
+        loop(nn, mine)
+
+        def send(i):
+            to = lax.rem(c + i + 1, nc)
+            remote(cs.at[to], cr.at[c], css.at[to], crs.at[c], dev=to * 2 + k).start()
+
+        loop(nc - 1, send)
+
+        def take(i):
+            frm = lax.rem(c + i + 1, nc)
+            remote(cs.at[frm], cr.at[frm], css.at[frm], crs.at[frm], dev=frm * 2 + k).wait_recv()
+
+        loop(nc - 1, take)
+        for n in range(nn):
+            v = pown[n, c]
+            for i in range(1, nc):
+                v = v + cr[lax.rem(c + i, nc), n].astype(F32)
+            finish(n, v)
+
+        def done_pair(n):
+            remote(ps.at[n], pr.at[n], pss.at[n], prs.at[n], dev=pair).wait_send()
+
+        def done(i):
+            to = lax.rem(c + i + 1, nc)
+            remote(cs.at[to], cr.at[c], css.at[to], crs.at[c], dev=to * 2 + k).wait_send()
+
+        def drain():
+            loop(nn, done_pair)
+            loop(nc - 1, done)
+
+        return drain
+
+    rcopy.wait()
+
+    def finish_x(n, v):
+        cols = pl.ds(pl.multiple_of(k * half + n * 512, 512), 512)
+        for h in range(2):
+            xf[n, 4 * h:4 * h + 4, :] = rbuf[h, :, cols].astype(F32)
+        v = v + xf[n]
+        xf[n] = v
+        xall[k, c, n] = (v * gain_ref[:, cols]).astype(BF16)
+
+    drain1 = reduce_rows(lhs, wo, psend, prec, csend, crecv, p1s, p1r, c1s, c1r, finish_x)
+
+    def ag_send(i):
+        to = lax.rem(c + i + 1, nc)
+        remote(xall.at[k, c], xall.at[k, c], ags.at[to], agr.at[c], dev=to * 2 + k).start()
+
+    loop(nc - 1, ag_send)
+
+    def forward(frm):
+        return remote(xall.at[k, frm], xall.at[k, frm], fws.at[frm], fwr.at[frm], dev=pair)
+
+    forward(c).start()
+
+    def ag_take(i):
+        frm = lax.rem(c + i + 1, nc)
+        remote(xall.at[k, frm], xall.at[k, frm], ags.at[frm], agr.at[frm], dev=frm * 2 + k).wait_recv()
+        forward(frm).start()
+
+    loop(nc - 1, ag_take)
+    drain1()
+
+    def fw_take(i):
+        remote(xall.at[ok, i], xall.at[ok, i], fws.at[i], fwr.at[i], dev=pair).wait_recv()
+
+    loop(nc, fw_take)
+
+    squares = jnp.zeros((rows, 128), F32)
+    for h in range(2):
+        for n in range(nn):
+            v = xall[h, :, n].astype(F32).reshape(rows, 512)
+            lo = h * half + n * 512
+            xg[:, lo:lo + 512] = v.astype(BF16)
+            v = v / gain_ref[:, lo:lo + 512]
+            v = v * v
+            for t in range(4):
+                squares = squares + v[:, t * 128:(t + 1) * 128]
+    ssq[g] = squares
+    scopy = remote(ssq.at[g], ssq.at[g], xs.at[2], xs.at[3], grp=og)
+    scopy.start()
+
+    def gate_up(base, n):
+        cols = pl.ds(pl.multiple_of(base + n * 128, 128), 128)
+        both = jnp.concatenate([wg[:, cols], wu[:, cols]], axis=1)
+        return jnp.dot(xg[...], both, preferred_element_type=F32)
+
+    def gcopy(n):
+        return remote(gsend.at[n], grecv.at[n], gs.at[n], gr.at[n], grp=og)
+
+    def hcopy(n):
+        return remote(hid.at[g, n], hid.at[g, n], hs.at[n], hr.at[n], grp=og)
+
+    for cp in gu_copies[0]:
+        cp.wait()
+
+    def for_other(n):
+        gsend[n] = gate_up(og * units, n).astype(BF16)
+        gcopy(n).start()
+
+    loop(nu, for_other)
+    for cp in gu_copies[1]:
+        cp.wait()
+    scopy.wait()
+    sums = jnp.sum(ssq[0] + ssq[1], axis=1, keepdims=True)
+    ssq[0] = jnp.broadcast_to(lax.rsqrt(sums / width_all + 1e-05), (rows, 128))
+
+    def for_me(n):
+        v = gate_up(g * units, n)
+        gcopy(n).wait_recv()
+        v = v + grecv[n].astype(F32)
+        gate = v[:, :128] * ssq[0]
+        up = v[:, 128:] * ssq[0]
+        hid[g, n] = (gate / (1.0 + jnp.exp(-gate)) * up).astype(BF16)
+        hcopy(n).start()
+
+    loop(nu, for_me)
+    wd_copy.wait()
+
+    def settle(n):
+        remote(hid.at[og, n], hid.at[og, n], hs.at[n], hr.at[n], grp=og).wait_recv()
+        gcopy(n).wait_send()
+        hcopy(n).wait_send()
+
+    loop(nu, settle)
+    for h in range(2):
+        for n in range(nu):
+            lo = h * units + n * 128
+            hcat[:, lo:lo + 128] = hid[h, n]
+
+    def finish_y(n, v):
+        v = v + xf[n]
+        xf[n] = v
+
+    drain2 = reduce_rows(hcat, wd, psend2, prec2, csend2, crecv2, p2s, p2r, c2s, c2r, finish_y)
+    for n in range(nn):
+        for h in range(2):
+            fin[h, :, n * 512:(n + 1) * 512] = xf[n, 4 * h:4 * h + 4, :].astype(BF16)
+    fcopy = remote(fin.at[ok], out_ref.at[k], fs.at[0], fs.at[1], dev=pair)
+    fcopy.start()
+    out_ref[k] = fin[k]
+
+    def done_attn(i):
+        to = lax.rem(d + i + 1, nd)
+        remote(abuf.at[:, to], arecv.at[d], as_.at[to], ar.at[d], dev=to).wait_send()
+
+    loop(nd - 1, done_attn)
+
+    def done_gather(i):
+        to = lax.rem(c + i + 1, nc)
+        remote(xall.at[k, c], xall.at[k, c], ags.at[to], agr.at[c], dev=to * 2 + k).wait_send()
+
+    loop(nc - 1, done_gather)
+
+    def done_forward(i):
+        forward(i).wait_send()
+
+    loop(nc, done_forward)
+    drain2()
+    fcopy.wait()
+
+
+def fused_device(
+    nd, query, key_cache, value_cache, lengths, out_weight, resid, norm_gain,
+    gate_weight, up_weight, down_weight,
+):
+    nc = nd // 2
+    rows = nd * 4
+    heads = query.shape[1]
+    ctx, kvh, hd = key_cache.shape[1:]
+    slots = ctx * kvh
+    wide = out_weight.shape[1]
+    half = wide // 2
+    nn = half // 512
+    ff = gate_weight.shape[1]
+    nu = ff // 256
+    keys = key_cache.reshape(2, slots, hd)
+    values = value_cache.reshape(2, slots, hd)
+    gain = norm_gain.astype(F32).reshape(1, wide)
+    vm = pl.BlockSpec(memory_space=pltpu.VMEM)
+    hbm = pl.BlockSpec(memory_space=pl.ANY)
+    sm = pl.BlockSpec(memory_space=pltpu.SMEM)
+    V = pltpu.VMEM
+    dma = lambda n: pltpu.SemaphoreType.DMA((n,))
+    out = pl.pallas_call(
+        functools.partial(layer_kernel, nd),
+        out_shape=jax.ShapeDtypeStruct((2, 4, half), BF16),
+        in_specs=[sm, vm, hbm, hbm, hbm, vm, vm, hbm, hbm, hbm],
+        out_specs=vm,
+        scratch_shapes=[
+            V((2, slots, hd), BF16), V((2, slots, hd), BF16),
+            V(out_weight.shape, BF16), V(gate_weight.shape, BF16),
+            V(up_weight.shape, BF16), V(down_weight.shape, BF16),
+            V((heads, slots), F32), V((nd, 8, 128), F32), V((2, nd, 8, 128), BF16),
+            V((nd, 2, 8, 128), BF16), V((2 * nd * 8, 128), F32),
+            V((rows, 512), BF16), V((2, 4, wide), BF16),
+            V((nn, nc, 8, 512), BF16), V((nn, nc, 8, 512), BF16), V((nn, nc, 8, 512), F32),
+            V((nc, nn, 8, 512), BF16), V((nc, nn, 8, 512), BF16), V((nn, 8, 512), F32),
+            V((2, nc, nn, 8, 512), BF16), V((rows, wide), BF16), V((2, rows, 128), F32),
+            V((nu, rows, 256), BF16), V((nu, rows, 256), BF16),
+            V((2, nu, rows, 128), BF16), V((rows, ff), BF16),
+            V((nn, nc, 8, 512), BF16), V((nn, nc, 8, 512), BF16),
+            V((nc, nn, 8, 512), BF16), V((nc, nn, 8, 512), BF16), V((2, 4, half), BF16),
+            dma(4), dma(6), dma(4), dma(2), dma(nd), dma(nd), dma(nn), dma(nn), dma(nc), dma(nc),
+            dma(nc), dma(nc), dma(nc), dma(nc), dma(nu), dma(nu), dma(nu), dma(nu),
+            dma(nn), dma(nn), dma(nc), dma(nc), dma(2),
+        ],
+        compiler_params=pltpu.CompilerParams(
+            collective_id=0, has_side_effects=True, vmem_limit_bytes=63 * 1024 * 1024
+        ),
+        name="decode_layer",
+    )(lengths, query, keys, values, out_weight, resid, gain, gate_weight, up_weight, down_weight)
+    return jnp.concatenate([out[0], out[1]], axis=1)
+
+
+def fits(mesh):
+    return mesh.shape["grp"] == 2 and mesh.shape["dev"] == 16
+
+
+def chosen(nd, use, *args):
+    query, out_weight, gate_weight = args[0], args[4], args[7]
+    same = (
+        use and query.shape == (2, 64, 128) and out_weight.shape == (512, 4096)
+        and gate_weight.shape[1] % 256 == 0
+    )
+    return fused_device(nd, *args) if same else per_device(*args)
+
+
 def solution(mesh):
     placed = (
         P(("grp", "dev"), None, None),
@@ -85,5 +475,5 @@
         P("dev", "grp"),
     )
     return jax.shard_map(
-        per_device, mesh=mesh, in_specs=placed, out_specs=P("dev", "grp"), check_vma=False
-    )
+        functools.partial(chosen, mesh.shape["dev"], fits(mesh)), mesh=mesh, in_specs=placed, out_specs=P("dev", "grp"), check_vma=False
+    )

time: 348 us -> 58.8 us (0.17)
  waiting for transfers between devices: 266 us -> 0 us
  Pallas kernels: 0 us -> 55.8 us
  matrix products: 32.1 us -> 0 us
  blocking collectives: 26 us -> 0 us
  between operations: 13.9 us -> 0.01 us
  other arithmetic: 6.65 us -> 1.94 us
    unnamed x6 -> x0, waiting for transfers between devices: 185 us -> none
    all_gather x1 -> x0, waiting for transfers between devices: 56.5 us -> none  [per_device(): lax.all_gather(attn, ('grp', 'dev'), axis=0, tiled=True)]
    pallas_call x0 -> x1, Pallas kernels: none -> 55.8 us  [fused_device(): pl.pallas_call(functools.partial(layer_kernel, nd), out_shape=jax.ShapeDt...]
    dot_general x6 -> x0, matrix products: 32.1 us -> none  [the longest x1 8.84 us: per_device(): jnp.dot(hidden, down_weight, preferred_element_type=jnp.float32)]
    psum x1 -> x0, waiting for transfers between devices: 24.5 us -> none  [per_device(): both = lax.psum(half_terms.astype(jnp.bfloat16), 'grp').astype(jnp.float32)]
    all_gather x1 -> x0, blocking collectives: 21.1 us -> none  [per_device(): piece = lax.all_gather(normed, 'dev', axis=0, tiled=True)]
    psum x1 -> x0, blocking collectives: 4.94 us -> none  [per_device(): sumsq = lax.psum(jnp.sum(x * x, axis=1), 'grp')]
    unnamed x12 -> x0, local copies, waits for them, and re-layouts: 3.56 us -> none
  transfers between devices with their start and end apart: 4 -> 0, of which waited for: 4 -> 0; matrix products, arithmetic and copies ran while one was open for 0% -> 0% of each run, Pallas kernels for 0% -> 0%
where the time goes in v1:
time: 58.8 us; the launch traced here: 58.5 us
  Pallas kernels  55.8 us (95%)
  other arithmetic  1.94 us (3%)
  local copies, waits for them, and re-layouts  0.75 us (1%)
    pallas_call x1, Pallas kernels, fused_device(): pl.pallas_call(functools.partial(layer_kernel, nd), out_shape=jax.ShapeDt...  55.8 us
    reshape x1, other arithmetic, fused_device(): gain = norm_gain.astype(F32).reshape(1, wide)  1.3 us

profile of v1, /device:TPU:0, one launch (start us, length us, event | category | flops | bytes accessed | tf_op | source)
XLA Modules:
  0.0 58.5 jit_solution(2445940141230705505)
XLA Ops:
  0.0 1.3 %reshape.15 = f32[4096]{0:T(1024)} convert(bf16[4096]{0:T(1024)(128)(2,1)} %param.16) | non-fusion elementwise | flops 4096 | bytes 24576 | tf_op jit(solution)/shard_map/reshape | solution.py:414
  1.3 55.8 %decode_layer.1 = bf16[2,4,2048]{2,1,0:T(4,128)(2,1)} custom-call(s32[2]{0:T(128)} %len_ref.1, bf16[2,64,128]{2,1,0:T(8,128)(2,1)} %q_ref.1, bf16[2,4096,128]{2,1,0:T(8,128)(2,1)} %bitcast.7, bf16[2,4096,128]{2,1,0:T(8,128)(2,1)} %bitcast.8, bf16[512,4096]{1,0:T(8,128)(2,1)} %wo_hbm.1, bf16[4,4096]{1,0:T(4,128)(2,1)} %resid_ref.1, f32[1,4096]{1,0:T(1,128)} %bitcast.9, ...), custom_call_target="tpu_custom_call" | custom-call | tf_op jit(solution)/shard_map/decode_layer/pallas_call | solution.py:420
  57.1 0.8 %slice_bitcast_fusion.1 = (bf16[4,2048]{1,0:T(4,128)(2,1)S(1)}, bf16[4,2048]{1,0:T(4,128)(2,1)S(1)}) fusion(bf16[2,4,2048]{2,1,0:T(4,128)(2,1)} %decode_layer.1), kind=kLoop, calls=%fused_computation.2 | loop fusion | bytes 65536 | tf_op jit(solution)/shard_map/squeeze | solution.py:448
  57.8 0.6 %pad_maximum_fusion = bf16[4,4096]{1,0:T(4,128)(2,1)} fusion(bf16[4,2048]{1,0:T(4,128)(2,1)S(1)} %get-tuple-element.6, bf16[4,2048]{1,0:T(4,128)(2,1)S(1)} %get-tuple-element.5), kind=kLoop, calls=%fused_computation | loop fusion | flops 65536 | bytes 65536 | tf_op jit(solution)/shard_map/concatenate | solution.py:448

commit v2 on v1

--- a/solution.py
+++ b/solution.py
@@ -103,7 +103,7 @@
     psend, prec, pown, csend, crecv, xf, xall, xg, ssq,
     gsend, grecv, hid, hcat,
     psend2, prec2, csend2, crecv2, fin,
-    kvsem, wsem, xs, rs, as_, ar, p1s, p1r, c1s, c1r, ags, agr, fws, fwr,
+    kvsem, wsem, xs, rs, as_, ar, p1s, p1r, c1s, c1r, ags, agr, fws, fwr, ys, yr,
     gs, gr, hs, hr, p2s, p2r, c2s, c2r, fs,
 ):
     nc = nd // 2
@@ -124,14 +124,20 @@
     width_all = wo.shape[1] * 2
 
     barrier = pltpu.get_barrier_semaphore()
-    pl.semaphore_signal(barrier, inc=1, device_id={"grp": og}, device_id_type=MESH)
+    all_ = 2 * nd
+    me = g * nd + d
+
+    def peer(i):
+        t = lax.rem(me + i + 1, all_)
+        return t, t // nd, lax.rem(t, nd)
 
     def greet(i):
+        t, tg, td = peer(i)
         pl.semaphore_signal(
-            barrier, inc=1, device_id={"dev": lax.rem(d + i + 1, nd)}, device_id_type=MESH
+            barrier, inc=1, device_id={"grp": tg, "dev": td}, device_id_type=MESH
         )
 
-    loop(nd - 1, greet)
+    loop(all_ - 1, greet)
 
     kv = []
     for r in range(2):
@@ -159,17 +165,17 @@
         kv[r][0].wait()
         q = q_ref[r]
         length = len_ref[r]
-        row_head = lax.broadcasted_iota(jnp.int32, (heads, piece), 0) // 8
+        row_head = lax.broadcasted_iota(jnp.int32, (heads, piece), 0) >> 3
         col = lax.broadcasted_iota(jnp.int32, (heads, piece), 1)
-        own = lax.rem(col, 8) == row_head
-        place = col // 8
+        own = (col & 7) == row_head
+        place = jnp.where(own, col >> 3, slots)
         top = jnp.full((heads, 1), -1e30, F32)
         for n in range(np_):
             s = lax.dot_general(
                 q, kb[r, n * piece:(n + 1) * piece, :], (((1,), (1,)), ((), ())),
                 preferred_element_type=F32,
             ) * (128 ** -0.5)
-            live = own & (place + n * (piece // 8) < length)
+            live = place < length - n * (piece // 8)
             s = jnp.where(live, s, -1e30)
             sc[:, n * piece:(n + 1) * piece] = s
             top = jnp.maximum(top, jnp.max(s, axis=1, keepdims=True))
@@ -188,31 +194,27 @@
         o = o / total
         for t in range(nd):
             ast[t, 4 * r:4 * r + 4, :] = o[4 * t:4 * t + 4, :]
-    abuf[g] = ast[...].astype(BF16)
-
-    pl.semaphore_wait(barrier, nd)
-    xcopy = remote(abuf.at[g], abuf.at[g], xs.at[0], xs.at[1], grp=og)
-    xcopy.start()
+    abuf[...] = ast[...].astype(BF16)
+
+    pl.semaphore_wait(barrier, all_ - 1)
+
+    def send_attn(i):
+        t, tg, td = peer(i)
+        remote(abuf.at[td], arecv.at[me], as_.at[t], ar.at[me], grp=tg, dev=td).start()
+
+    loop(all_ - 1, send_attn)
     rcopy = remote(resid_ref, rbuf.at[k], rs.at[0], rs.at[1], dev=pair)
     rcopy.start()
     rbuf[k] = resid_ref[...]
-    xcopy.wait()
-
-    def send_attn(i):
-        to = lax.rem(d + i + 1, nd)
-        remote(abuf.at[:, to], arecv.at[d], as_.at[to], ar.at[d], dev=to).start()
-
-    loop(nd - 1, send_attn)
-    arecv[d] = abuf[:, d]
+    arecv[me] = abuf[d]
 
     def take_attn(i):
-        frm = lax.rem(d + i + 1, nd)
-        remote(abuf.at[:, frm], arecv.at[frm], as_.at[frm], ar.at[frm], dev=frm).wait_recv()
-
-    loop(nd - 1, take_attn)
+        t, tg, td = peer(i)
+        remote(abuf.at[td], arecv.at[t], as_.at[t], ar.at[t], grp=tg, dev=td).wait_recv()
+
+    loop(all_ - 1, take_attn)
     wo_copy.wait()
-    for h in range(2):
-        af[h * nd * 8:(h + 1) * nd * 8, :] = arecv[:, h].astype(F32).reshape(nd * 8, 128)
+    af[...] = arecv[...].astype(F32).reshape(all_ * 8, 128)
     for j in range(4):
         lhs[:, j * 128:(j + 1) * 128] = af[pl.ds(j, rows, stride=4), :].astype(BF16)
 
@@ -223,7 +225,16 @@
             ps[n] = v.reshape(nc, 8, 512).astype(BF16)
             remote(ps.at[n], pr.at[n], pss.at[n], prs.at[n], dev=pair).start()
 
-        loop(nn, other)
+        def part(n, to):
+            return remote(
+                cs.at[n, to], cr.at[n, c], css.at[n * nc + to], crs.at[n * nc + c], dev=to * 2 + k
+            )
+
+        def arrived(n, frm):
+            return remote(
+                cs.at[n, frm], cr.at[n, frm], css.at[n * nc + frm], crs.at[n * nc + frm],
+                dev=frm * 2 + k,
+            )
 
         def mine(n):
             cols = pl.ds(pl.multiple_of(k * half + n * 512, 512), 512)
@@ -231,41 +242,54 @@
             remote(ps.at[n], pr.at[n], pss.at[n], prs.at[n], dev=pair).wait_recv()
             v = v.reshape(nc, 8, 512) + pr[n].astype(F32)
             pown[n] = v
-            cs[:, n] = v.astype(BF16)
-
-        loop(nn, mine)
-
-        def send(i):
-            to = lax.rem(c + i + 1, nc)
-            remote(cs.at[to], cr.at[c], css.at[to], crs.at[c], dev=to * 2 + k).start()
-
-        loop(nc - 1, send)
-
-        def take(i):
-            frm = lax.rem(c + i + 1, nc)
-            remote(cs.at[frm], cr.at[frm], css.at[frm], crs.at[frm], dev=frm * 2 + k).wait_recv()
-
-        loop(nc - 1, take)
-        for n in range(nn):
+            cs[n] = v.astype(BF16)
+            loop(nc - 1, lambda i: part(n, lax.rem(c + i + 1, nc)).start())
+
+        def both(n):
+            other(n + 1)
+            mine(n)
+
+        other(0)
+        loop(nn - 1, both)
+        mine(nn - 1)
+
+        def total(n):
+            loop(nc - 1, lambda i: arrived(n, lax.rem(c + i + 1, nc)).wait_recv())
             v = pown[n, c]
             for i in range(1, nc):
-                v = v + cr[lax.rem(c + i, nc), n].astype(F32)
+                v = v + cr[n, lax.rem(c + i, nc)].astype(F32)
             finish(n, v)
+
+        loop(nn, total)
 
         def done_pair(n):
             remote(ps.at[n], pr.at[n], pss.at[n], prs.at[n], dev=pair).wait_send()
 
-        def done(i):
-            to = lax.rem(c + i + 1, nc)
-            remote(cs.at[to], cr.at[c], css.at[to], crs.at[c], dev=to * 2 + k).wait_send()
+        def done(j):
+            part(j // (nc - 1), lax.rem(c + 1 + lax.rem(j, nc - 1), nc)).wait_send()
 
         def drain():
             loop(nn, done_pair)
-            loop(nc - 1, done)
+            loop(nn * (nc - 1), done)
 
         return drain
 
     rcopy.wait()
+
+    nz = nc // 2
+    yc = c + 1 - 2 * lax.rem(c, 2)
+
+    def along_z(n, to):
+        return remote(xall.at[k, n, c], xall.at[k, n, c], ags.at[n * nc + to], agr.at[n * nc + c], dev=to * 2 + k)
+
+    def from_z(n, frm):
+        return remote(xall.at[k, n, frm], xall.at[k, n, frm], ags.at[n * nc + frm], agr.at[n * nc + frm], dev=frm * 2 + k)
+
+    def along_y(n, frm):
+        return remote(xall.at[k, n, frm], xall.at[k, n, frm], ys.at[n * nc + frm], yr.at[n * nc + frm], dev=yc * 2 + k)
+
+    def forward(n, frm):
+        return remote(xall.at[k, n, frm], xall.at[k, n, frm], fws.at[n * nc + frm], fwr.at[n * nc + frm], dev=pair)
 
     def finish_x(n, v):
         cols = pl.ds(pl.multiple_of(k * half + n * 512, 512), 512)
@@ -273,45 +297,59 @@
             xf[n, 4 * h:4 * h + 4, :] = rbuf[h, :, cols].astype(F32)
         v = v + xf[n]
         xf[n] = v
-        xall[k, c, n] = (v * gain_ref[:, cols]).astype(BF16)
+        xall[k, n, c] = (v * gain_ref[:, cols].astype(F32)).astype(BF16)
+        loop(nz - 1, lambda i: along_z(n, lax.rem(c + 2 * i + 2, nc)).start())
+        along_y(n, c).start()
+        forward(n, c).start()
 
     drain1 = reduce_rows(lhs, wo, psend, prec, csend, crecv, p1s, p1r, c1s, c1r, finish_x)
 
-    def ag_send(i):
-        to = lax.rem(c + i + 1, nc)
-        remote(xall.at[k, c], xall.at[k, c], ags.at[to], agr.at[c], dev=to * 2 + k).start()
-
-    loop(nc - 1, ag_send)
-
-    def forward(frm):
-        return remote(xall.at[k, frm], xall.at[k, frm], fws.at[frm], fwr.at[frm], dev=pair)
-
-    forward(c).start()
-
-    def ag_take(i):
-        frm = lax.rem(c + i + 1, nc)
-        remote(xall.at[k, frm], xall.at[k, frm], ags.at[frm], agr.at[frm], dev=frm * 2 + k).wait_recv()
-        forward(frm).start()
-
-    loop(nc - 1, ag_take)
+    def z_take(n):
+        def one(i):
+            frm = lax.rem(c + 2 * i + 2, nc)
+            from_z(n, frm).wait_recv()
+            along_y(n, frm).start()
+            forward(n, frm).start()
+
+        loop(nz - 1, one)
+
+    def y_take(n):
+        def one(i):
+            frm = lax.rem(yc + 2 * i, nc)
+            along_y(n, frm).wait_recv()
+            forward(n, frm).start()
+
+        loop(nz, one)
+
+    def build(h, n):
+        cols = pl.ds(pl.multiple_of(h * half + n * 512, 512), 512)
+        v = xall[h, n].astype(F32).reshape(rows, 512)
+        xg[:, cols] = v.astype(BF16)
+        v = v * (1.0 / gain_ref[:, cols].astype(F32))
+        v = v * v
+        ssq[g] += (v[:, :128] + v[:, 128:256]) + (v[:, 256:384] + v[:, 384:])
+
+    ssq[g] = jnp.zeros((rows, 128), F32)
+    z_take(0)
+
+    def stage(n):
+        z_take(n + 1)
+        y_take(n)
+        build(k, n)
+
+    loop(nn - 1, stage)
+    y_take(nn - 1)
+    build(k, nn - 1)
+
+    def pair_half(n):
+        def one(i):
+            remote(xall.at[ok, n, i], xall.at[ok, n, i], fws.at[n * nc + i], fwr.at[n * nc + i], dev=pair).wait_recv()
+
+        loop(nc, one)
+        build(ok, n)
+
+    loop(nn, pair_half)
     drain1()
-
-    def fw_take(i):
-        remote(xall.at[ok, i], xall.at[ok, i], fws.at[i], fwr.at[i], dev=pair).wait_recv()
-
-    loop(nc, fw_take)
-
-    squares = jnp.zeros((rows, 128), F32)
-    for h in range(2):
-        for n in range(nn):
-            v = xall[h, :, n].astype(F32).reshape(rows, 512)
-            lo = h * half + n * 512
-            xg[:, lo:lo + 512] = v.astype(BF16)
-            v = v / gain_ref[:, lo:lo + 512]
-            v = v * v
-            for t in range(4):
-                squares = squares + v[:, t * 128:(t + 1) * 128]
-    ssq[g] = squares
     scopy = remote(ssq.at[g], ssq.at[g], xs.at[2], xs.at[3], grp=og)
     scopy.start()
 
@@ -371,26 +409,23 @@
     for n in range(nn):
         for h in range(2):
             fin[h, :, n * 512:(n + 1) * 512] = xf[n, 4 * h:4 * h + 4, :].astype(BF16)
-    fcopy = remote(fin.at[ok], out_ref.at[k], fs.at[0], fs.at[1], dev=pair)
+    mycols = pl.ds(pl.multiple_of(k * half, 512), half)
+    fcopy = remote(fin.at[ok], out_ref.at[:, mycols], fs.at[0], fs.at[1], dev=pair)
     fcopy.start()
-    out_ref[k] = fin[k]
+    out_ref[:, mycols] = fin[k]
 
     def done_attn(i):
-        to = lax.rem(d + i + 1, nd)
-        remote(abuf.at[:, to], arecv.at[d], as_.at[to], ar.at[d], dev=to).wait_send()
-
-    loop(nd - 1, done_attn)
-
-    def done_gather(i):
-        to = lax.rem(c + i + 1, nc)
-        remote(xall.at[k, c], xall.at[k, c], ags.at[to], agr.at[c], dev=to * 2 + k).wait_send()
-
-    loop(nc - 1, done_gather)
-
-    def done_forward(i):
-        forward(i).wait_send()
-
-    loop(nc, done_forward)
+        t, tg, td = peer(i)
+        remote(abuf.at[td], arecv.at[me], as_.at[t], ar.at[me], grp=tg, dev=td).wait_send()
+
+    loop(all_ - 1, done_attn)
+
+    def done_gather(n):
+        loop(nz - 1, lambda i: along_z(n, lax.rem(c + 2 * i + 2, nc)).wait_send())
+        loop(nz, lambda i: along_y(n, lax.rem(c + 2 * i, nc)).wait_send())
+        loop(nc, lambda i: forward(n, i).wait_send())
+
+    loop(nn, done_gather)
     drain2()
     fcopy.wait()
 
@@ -411,7 +446,7 @@
     nu = ff // 256
     keys = key_cache.reshape(2, slots, hd)
     values = value_cache.reshape(2, slots, hd)
-    gain = norm_gain.astype(F32).reshape(1, wide)
+    gain = norm_gain.reshape(1, wide)
     vm = pl.BlockSpec(memory_space=pltpu.VMEM)
     hbm = pl.BlockSpec(memory_space=pl.ANY)
     sm = pl.BlockSpec(memory_space=pltpu.SMEM)
@@ -419,33 +454,33 @@
     dma = lambda n: pltpu.SemaphoreType.DMA((n,))
     out = pl.pallas_call(
         functools.partial(layer_kernel, nd),
-        out_shape=jax.ShapeDtypeStruct((2, 4, half), BF16),
+        out_shape=jax.ShapeDtypeStruct((4, wide), BF16),
         in_specs=[sm, vm, hbm, hbm, hbm, vm, vm, hbm, hbm, hbm],
         out_specs=vm,
         scratch_shapes=[
             V((2, slots, hd), BF16), V((2, slots, hd), BF16),
             V(out_weight.shape, BF16), V(gate_weight.shape, BF16),
             V(up_weight.shape, BF16), V(down_weight.shape, BF16),
-            V((heads, slots), F32), V((nd, 8, 128), F32), V((2, nd, 8, 128), BF16),
-            V((nd, 2, 8, 128), BF16), V((2 * nd * 8, 128), F32),
+            V((heads, slots), F32), V((nd, 8, 128), F32), V((nd, 8, 128), BF16),
+            V((2 * nd, 8, 128), BF16), V((2 * nd * 8, 128), F32),
             V((rows, 512), BF16), V((2, 4, wide), BF16),
             V((nn, nc, 8, 512), BF16), V((nn, nc, 8, 512), BF16), V((nn, nc, 8, 512), F32),
-            V((nc, nn, 8, 512), BF16), V((nc, nn, 8, 512), BF16), V((nn, 8, 512), F32),
-            V((2, nc, nn, 8, 512), BF16), V((rows, wide), BF16), V((2, rows, 128), F32),
+            V((nn, nc, 8, 512), BF16), V((nn, nc, 8, 512), BF16), V((nn, 8, 512), F32),
+            V((2, nn, nc, 8, 512), BF16), V((rows, wide), BF16), V((2, rows, 128), F32),
             V((nu, rows, 256), BF16), V((nu, rows, 256), BF16),
             V((2, nu, rows, 128), BF16), V((rows, ff), BF16),
             V((nn, nc, 8, 512), BF16), V((nn, nc, 8, 512), BF16),
-            V((nc, nn, 8, 512), BF16), V((nc, nn, 8, 512), BF16), V((2, 4, half), BF16),
-            dma(4), dma(6), dma(4), dma(2), dma(nd), dma(nd), dma(nn), dma(nn), dma(nc), dma(nc),
-            dma(nc), dma(nc), dma(nc), dma(nc), dma(nu), dma(nu), dma(nu), dma(nu),
-            dma(nn), dma(nn), dma(nc), dma(nc), dma(2),
+            V((nn, nc, 8, 512), BF16), V((nn, nc, 8, 512), BF16), V((2, 4, half), BF16),
+            dma(4), dma(6), dma(4), dma(2), dma(2 * nd), dma(2 * nd), dma(nn), dma(nn),
+            *[dma(nn * nc) for _ in range(8)], dma(nu), dma(nu), dma(nu), dma(nu),
+            dma(nn), dma(nn), dma(nn * nc), dma(nn * nc), dma(2),
         ],
         compiler_params=pltpu.CompilerParams(
             collective_id=0, has_side_effects=True, vmem_limit_bytes=63 * 1024 * 1024
         ),
         name="decode_layer",
     )(lengths, query, keys, values, out_weight, resid, gain, gate_weight, up_weight, down_weight)
-    return jnp.concatenate([out[0], out[1]], axis=1)
+    return out
 
 
 def fits(mesh):

time: 58.8 us -> 60.5 us (1.029)
  local copies, waits for them, and re-layouts: 0.75 us -> 2.7 us
  other arithmetic: 1.94 us -> 0 us
  Pallas kernels: 55.8 us -> 57.5 us
    pallas_call x1, Pallas kernels: 55.8 us -> 57.5 us  [fused_device(): pl.pallas_call(functools.partial(layer_kernel, nd), out_shape=jax.ShapeDt...]
    unnamed x0 -> x1, local copies, waits for them, and re-layouts: none -> 1.39 us
    reshape x0 -> x1, local copies, waits for them, and re-layouts: none -> 1.31 us  [fused_device(): gain = norm_gain.reshape(1, wide)]
    reshape x1 -> x0, other arithmetic: 1.3 us -> none  [fused_device(): gain = norm_gain.astype(F32).reshape(1, wide)]
    squeeze x1 -> x0, local copies, waits for them, and re-layouts: 0.75 us -> none  [fused_device(): return jnp.concatenate([out[0], out[1]], axis=1)]
    concatenate x1 -> x0, other arithmetic: 0.63 us -> none  [fused_device(): return jnp.concatenate([out[0], out[1]], axis=1)]
where the time goes in v2:
time: 60.5 us; the launch traced here: 60.2 us
  Pallas kernels  57.5 us (95%)
  local copies, waits for them, and re-layouts  2.7 us (4%)
    pallas_call x1, Pallas kernels, fused_device(): pl.pallas_call(functools.partial(layer_kernel, nd), out_shape=jax.ShapeDt...  57.5 us
    unnamed x1, local copies, waits for them, and re-layouts  1.39 us
    reshape x1, local copies, waits for them, and re-layouts, fused_device(): gain = norm_gain.reshape(1, wide)  1.31 us

profile of v2, /device:TPU:0, one launch (start us, length us, event | category | flops | bytes accessed | tf_op | source)
XLA Modules:
  0.0 60.2 jit_solution(5813931377410828895)
XLA Ops:
  0.0 1.3 %reshape.11.gain_ref = bf16[1,4096]{1,0:T(2,128)(2,1)} reshape(bf16[4096]{0:T(1024)(128)(2,1)} %param.16) | data formatting | bytes 16384 | tf_op jit(solution)/shard_map/reshape | solution.py:449
  1.3 57.5 %decode_layer.1 = bf16[4,4096]{1,0:T(4,128)(2,1)} custom-call(s32[2]{0:T(128)} %len_ref.1, bf16[2,64,128]{2,1,0:T(8,128)(2,1)} %q_ref.1, bf16[2,4096,128]{2,1,0:T(8,128)(2,1)} %bitcast.2, bf16[2,4096,128]{2,1,0:T(8,128)(2,1)} %bitcast.3, bf16[512,4096]{1,0:T(8,128)(2,1)} %wo_hbm.1, bf16[4,4096]{1,0:T(4,128)(2,1)} %resid_ref.1, ...), custom_call_target="tpu_custom_call" | custom-call | tf_op jit(solution)/shard_map/decode_layer/pallas_call | solution.py:455
  58.8 1.4 %copy.12 = bf16[4,4096]{1,0:T(4,128)(2,1)} copy(bf16[4,4096]{1,0:T(4,128)(2,1)} %decode_layer.1) | data formatting | bytes 65536
